TPU v7x, 128 devices: a whole 4x4x4 slice. The times are simulated.
128 devices in a mesh: tok: 8 (over z, core), feat: 16 (over x, y).
Axes of the slice: x: 4, y: 4, z: 4, core: 2. Of those that a mesh axis runs over, the one named last changes fastest.
Arguments:
- residual: bfloat16 [2, 2048, 3584], P(None, 'tok', 'feat'), may hold values from -6 to 6
- enc_weight: bfloat16 [2, 3584, 16384], P(None, None, 'feat'), may hold values from -0.09375 to 0.09375
- enc_bias: float32 [2, 16384], P(None, 'feat'), may hold values from -3 to 3
- dec_sum: bfloat16 [2, 16384, 3584], P(None, 'feat', 'tok'), may hold values from -0.09375 to 0.09375
- unembed: bfloat16 [131072, 3584], P(('tok', 'feat')), may hold values from -6 to 6
- norm_gain: float32 [3584], replicated, may hold values from 0.25 to 1.75
- target_ids: int32 [64], replicated, may hold values from 0 to 131071
- active_ids: int32 [2, 2048, 192], P(None, 'tok', 'feat'), may hold values from -1 to 16383, as said below
Outputs:
- edges: bfloat16 [2, 2048, 12288], P(None, ('tok', 'feat'))
Inputs may be any that keep to these rules, and one draw needn't show every extreme that they name: `active_ids`: slot group g of a token and layer (slots g * 12 to (g + 1) * 12 - 1) holds distinct features of g * 1024 to (g + 1) * 1024 - 1 in its first slots, at least one, and -1 in the rest; in every layer some group is full.
All inputs are finite; a program needn't handle non-finite values.
Results may differ from a plain program's by a relative error of at most 0.0058.
Values may be sent and summed in bfloat16 or wider, within the bound.
No kernel may reach another device: no remote copies, remote signals or barrier semaphores. Data moves between devices by JAX's collectives and lax.ppermute only.
A program may use at most 128 MiB of HBM per device.

v0:
```python
import jax
import jax.numpy as jnp
from jax import lax
from jax.sharding import PartitionSpec as P


def per_device(residual, enc_weight, enc_bias, dec_sum, unembed, norm_gain, target_ids, active_ids):
    n_feat = lax.axis_size("feat")
    feat_pos = lax.axis_index("feat")
    tok_pos = lax.axis_index("tok")
    vocab_rows = unembed.shape[0]
    first_row = (tok_pos * n_feat + feat_pos) * vocab_rows
    selector = (
        target_ids[:, None] - first_row == jnp.arange(vocab_rows, dtype=jnp.int32)[None, :]
    ).astype(jnp.bfloat16)
    partial_rows = jnp.dot(selector, unembed, preferred_element_type=jnp.float32)
    layers = residual.shape[0]
    feat_rows = enc_weight.shape[2]
    width_part = dec_sum.shape[2]
    whole_rows = lax.psum(partial_rows, ("tok", "feat"))
    directions = (whole_rows * norm_gain[None, :]).astype(jnp.bfloat16)
    direction_slice = lax.dynamic_slice_in_dim(directions, tok_pos * width_part, width_part, 1)
    targets = direction_slice.shape[0]
    score_terms = jnp.einsum(
        "lfd,td->lft", dec_sum, direction_slice, preferred_element_type=jnp.float32
    )
    score_terms = score_terms.reshape(layers, feat_rows * targets)
    scores = lax.psum(score_terms, "tok").astype(jnp.bfloat16)
    activations = []
    clamps = []
    for layer_idx in range(layers):
        weights_now = enc_weight[layer_idx]

        def accumulate(running, segment, offset, weights_now=weights_now):
            return jnp.dot(segment, weights_now, preferred_element_type=jnp.float32)

        starting_value = jnp.zeros((residual.shape[1], feat_rows), jnp.float32)
        preactivation = accumulate(
            starting_value,
            lax.all_gather(residual[layer_idx], "feat", axis=1, tiled=True),
            jnp.int32(0),
        )
        preactivation = preactivation + enc_bias[layer_idx][None, :]
        feature_ids = active_ids[layer_idx]
        is_live = feature_ids >= 0
        clipped_activation = jnp.where(is_live, feature_ids - feat_pos * feat_rows, 0)
        values = jnp.take_along_axis(preactivation, clipped_activation, axis=1)
        activations.append(jnp.where(is_live, values, jnp.zeros_like(values)))
        clamps.append(clipped_activation)
    activation = jnp.stack(activations)
    slots = active_ids.shape[2]
    full_table = lax.all_gather(scores, "feat", axis=1, tiled=True).reshape(
        layers, n_feat * feat_rows, targets
    )
    moved_vals = lax.all_to_all(activation, "feat", split_axis=1, concat_axis=2, tiled=True)
    moved_ids = lax.all_to_all(active_ids, "feat", split_axis=1, concat_axis=2, tiled=True)
    live_there = moved_ids >= 0
    clamped_there = jnp.where(live_there, moved_ids, 0)
    blocks = []
    for layer_idx in range(layers):
        picked = jnp.take(full_table[layer_idx], clamped_there[layer_idx], axis=0).astype(
            jnp.float32
        )
        edge_vals = (moved_vals[layer_idx][:, :, None] * picked).astype(jnp.bfloat16)
        blocks.append(edge_vals.reshape(edge_vals.shape[0], n_feat * slots * targets))
    return jnp.stack(blocks)


def solution(mesh):
    return jax.shard_map(
        per_device,
        mesh=mesh,
        in_specs=(
            P(None, "tok", "feat"),
            P(None, None, "feat"),
            P(None, "feat"),
            P(None, "feat", "tok"),
            P(("tok", "feat"), None),
            P(),
            P(),
            P(None, "tok", "feat"),
        ),
        out_specs=P(None, ("tok", "feat"), None),
        check_vma=False,
    )
```

profile of v0, /device:TPU:0, one launch (start us, length us, event | category | flops | bytes accessed | tf_op | source)
XLA Modules:
  0.0 387.2 jit_solution(13353083011878141911)
XLA Ops:
  7.4 0.8 broadcast_subtract_fusion
  8.2 5.5 %fusion.18 = f32[64,3584]{1,0:T(8,128)} fusion(bf16[1024,3584]{1,0:T(8,128)(2,1)} %param.16, s32[64]{0:T(128)S(1)} %broadcast_subtract_fusion), kind=kOutput, calls=%fused_computation.22 | convolution fusion | flops 469827584 | bytes 8257792 | tf_op jit(solution)/shard_map/dot_general | solution.py:16
  15.9 149.1 %all-reduce.3.cloned.1.call-done = f32[64,3584]{1,0:T(8,128)} async-done(((f32[64,3584]{1,0:T(8,128)}), f32[64,3584]{1,0:T(8,128)}) %all-reduce.3.cloned.1.call-update) | async-done | bytes 917520 | tf_op jit(solution)/shard_map/psum | solution.py:20
  165.1 1.4 convolution_bitcast_fusion
  167.4 31.5 %all-reduce.4 = bf16[2,65536]{1,0:T(2,128)(2,1)} all-reduce(f32[2,65536]{1,0:T(2,128)S(1)} %reshape.38), channel_id=1, replica_groups=mesh['tok'=8,'feat'=16] {'tok'}, use_global_device_ids=true, to_apply=%region_1.3 | all-reduce | flops 131072 | bytes 786432 | tf_op jit(solution)/shard_map/psum | solution.py:28
  199.1 1.0 reshape.105
  200.1 5.3 %all-to-all-start.1 = ((s32[16,1,384]{2,1,0:T(1,128)}), s32[16,1,384]{2,1,0:T(1,128)S(1)}, u32[]{:S(2)}, u32[]{:S(2)}) async-start(s32[16,1,384]{2,1,0:T(1,128)} %reshape.105), calls=%async_computation.1 | async-start | bytes 49152 | tf_op jit(solution)/shard_map/all_to_all | solution.py:56
  205.9 7.2 %all-to-all-done.1 = s32[16,1,384]{2,1,0:T(1,128)S(1)} async-done(((s32[16,1,384]{2,1,0:T(1,128)}), s32[16,1,384]{2,1,0:T(1,128)S(1)}, u32[]{:S(2)}, u32[]{:S(2)}) %all-to-all-start.1) | async-done | bytes 24608 | tf_op jit(solution)/shard_map/all_to_all | solution.py:56
  215.4 5.8 %fusion.13 = f32[256,1024]{1,0:T(8,128)S(1)} fusion(bf16[2,3584,1024]{2,1,0:T(8,128)(2,1)} %param.13, bf16[1,256,3584]{1,2,0:T(8,128)(2,1)} %all-gather.10.cloned.1.call-done, f32[1024]{0:T(1024)S(1)} %bitcast.120), kind=kOutput, calls=%fused_computation.17 | convolution fusion | flops 1879310336 | bytes 10227712 | tf_op jit(solution)/shard_map/dot_general | solution.py:35
  221.2 24.7 %gather_fusion.1 = f32[3072]{0:T(1024)S(1)} fusion(f32[256,1024]{1,0:T(8,128)S(1)} %fusion.13, s32[3072]{0:T(1024)S(1)} %reshape.90), kind=kCustom, calls=%fused_computation.2.clone | custom fusion | bytes 49152 | tf_op jit(solution)/shard_map/jit(take_along_axis)/gather | solution.py:47
  246.2 5.7 %fusion.8 = f32[256,1024]{1,0:T(8,128)S(1)} fusion(bf16[2,3584,1024]{2,1,0:T(8,128)(2,1)} %param.13, bf16[1,256,3584]{1,2,0:T(8,128)(2,1)} %all-gather.8.cloned.1.call-done, f32[1024]{0:T(1024)S(1)} %bitcast.119), kind=kOutput, calls=%fused_computation.16 | convolution fusion | flops 1879310336 | bytes 10227712 | tf_op jit(solution)/shard_map/dot_general | solution.py:35
  251.9 24.7 %gather_fusion = f32[3072]{0:T(1024)S(1)} fusion(f32[256,1024]{1,0:T(8,128)S(1)} %fusion.8, s32[3072]{0:T(1024)S(1)} %reshape.85), kind=kCustom, calls=%fused_computation.clone | custom fusion | bytes 49152 | tf_op jit(solution)/shard_map/jit(take_along_axis)/gather | solution.py:47
  277.1 1.0 reshape.107
  278.1 3.7 all-to-all-start
  281.8 7.4 %all-to-all-done = f32[16,1,384]{2,1,0:T(1,128)S(1)} async-done(((f32[16,1,384]{2,1,0:T(1,128)}), f32[16,1,384]{2,1,0:T(1,128)S(1)}, u32[]{:S(2)}, u32[]{:S(2)}) %all-to-all-start) | async-done | bytes 24608 | tf_op jit(solution)/shard_map/all_to_all | solution.py:55
  291.8 47.4 %slice_reduce_fusion.1 = (bf16[1048576]{0:T(1024)(128)(2,1)}, bf16[1048576]{0:T(1024)(128)(2,1)}) fusion(bf16[2,1048576]{1,0:T(2,128)(2,1)} %all-gather.6.cloned.1.call-done), kind=kLoop, calls=%fused_computation.11 | loop fusion | bytes 8388608 | tf_op jit(solution)/shard_map/slice | solution.py:61
  339.2 6.1 %squeeze.32 = bf16[16384,64]{1,0:T(8,128)(2,1)} reshape(bf16[1048576]{0:T(1024)(128)(2,1)} %get-tuple-element.8) | data formatting | bytes 4194304 | tf_op jit(solution)/shard_map/squeeze | solution.py:61
  345.3 11.0 %gather_fusion.3 = bf16[3072,64]{1,0:T(8,128)(2,1)S(1)} fusion(bf16[16384,64]{1,0:T(8,128)(2,1)} %squeeze.32, s32[3072]{0:T(1024)S(1)} %broadcast_clamp_fusion), kind=kCustom, calls=%fused_computation.3.clone | custom fusion | bytes 798720 | tf_op jit(solution)/shard_map/jit(_take)/gather | solution.py:61
  356.3 1.1 multiply_convert_fusion
  357.4 1.4 stack_reshape.7
  358.8 6.1 %squeeze.30 = bf16[16384,64]{1,0:T(8,128)(2,1)} reshape(bf16[1048576]{0:T(1024)(128)(2,1)} %get-tuple-element.6) | data formatting | bytes 4194304 | tf_op jit(solution)/shard_map/squeeze | solution.py:61
  364.9 11.0 %gather_fusion.2 = bf16[3072,64]{1,0:T(8,128)(2,1)S(1)} fusion(bf16[16384,64]{1,0:T(8,128)(2,1)} %squeeze.30, s32[3072]{0:T(1024)S(1)} %broadcast_clamp_fusion.1), kind=kCustom, calls=%fused_computation.1.clone | custom fusion | bytes 798720 | tf_op jit(solution)/shard_map/jit(_take)/gather | solution.py:61
  375.9 1.1 multiply_convert_fusion.1
  377.6 1.9 pad_maximum_fusion
  (61 shorter events, 10.0 us)
Async XLA Ops:
  7.4 157.7 %copy-start = (bf16[2,1024,448]{1,2,0:T(8,128)(2,1)S(1)}, bf16[2,1024,448]{1,2,0:T(8,128)(2,1)}, u32[]{:S(2)}) copy-start(bf16[2,1024,448]{1,2,0:T(8,128)(2,1)} %param.15) | copy-start | bytes 5505028
  7.4 157.7 %all-reduce.3.cloned.1.call-start = ((), (), s32[]{:S(2)}) async-start(), calls=%async_computation.2 | async-start | bytes 1835008 | tf_op jit(solution)/shard_map/psum | solution.py:20
  8.2 5.6 %copy-start.1 = (bf16[2,256,224]{1,2,0:T(8,128)(2,1)S(1)}, bf16[2,256,224]{1,2,0:T(8,128)(2,1)}, u32[]{:S(2)}) copy-start(bf16[2,256,224]{1,2,0:T(8,128)(2,1)} %param.12) | copy-start | bytes 688132
  13.7 201.7 %all-gather.10.cloned.1.call-start = ((), (), s32[]{:S(2)}) async-start(), calls=%async_computation.5 | async-start | bytes 1949696 | tf_op jit(solution)/shard_map/all_gather | solution.py:40
  14.5 231.7 %all-gather.8.cloned.1.call-start = ((), (), s32[]{:S(2)}) async-start(), calls=%async_computation.4 | async-start | bytes 1949696 | tf_op jit(solution)/shard_map/all_gather | solution.py:40
  15.1 276.7 %all-gather.6.cloned.1.call-start = ((), (), s32[]{:S(2)}) async-start(), calls=%async_computation.3 | async-start | bytes 4456448 | tf_op jit(solution)/shard_map/all_gather | solution.py:52
  166.5 32.4 %copy-start.2 = (s32[2,256,12]{1,0,2:T(2,128)S(1)}, s32[2,256,12]{1,0,2:T(2,128)}, u32[]{:S(2)}) copy-start(s32[2,256,12]{1,0,2:T(2,128)} %param.19) | copy-start | bytes 73732
  166.5 39.0 %copy-start.3 = (f32[2,1024]{1,0:T(2,128)S(1)}, f32[2,1024]{1,0:T(2,128)}, u32[]{:S(2)}) copy-start(f32[2,1024]{1,0:T(2,128)} %param.14) | copy-start | bytes 24580
  200.1 13.1 %all-to-all-start.1 = ((s32[16,1,384]{2,1,0:T(1,128)}), s32[16,1,384]{2,1,0:T(1,128)S(1)}, u32[]{:S(2)}, u32[]{:S(2)}) async-start(s32[16,1,384]{2,1,0:T(1,128)} %reshape.105), calls=%async_computation.1 | async-start | bytes 49152 | tf_op jit(solution)/shard_map/all_to_all | solution.py:56
  278.1 11.0 %all-to-all-start = ((f32[16,1,384]{2,1,0:T(1,128)}), f32[16,1,384]{2,1,0:T(1,128)S(1)}, u32[]{:S(2)}, u32[]{:S(2)}) async-start(f32[16,1,384]{2,1,0:T(1,128)} %reshape.107), calls=%async_computation | async-start | bytes 49152 | tf_op jit(solution)/shard_map/all_to_all | solution.py:55
Sparse Core Ops, SparseCore 0:
  13.8 151.1 all-reduce.2
Sparse Core Ops, SparseCore 1:
  16.4 46.7 all-gather.9
  65.2 43.8 all-gather.7
  199.0 48.3 all-gather.5
where the time goes:
time: 388 us; the launch traced here: 387 us
  waiting for transfers between devices  164 us (42%)
  local copies, waits for them, and re-layouts  142 us (37%)
  blocking collectives  31.5 us (8%)
  matrix products  18.5 us (5%)
  between operations  15.4 us (4%)
  starting transfers between devices  9.12 us (2%)
  other arithmetic  6.43 us (2%)
    psum x1, waiting for transfers between devices, per_device(): whole_rows = lax.psum(partial_rows, ('tok', 'feat'))  149 us
    gather x10, local copies, waits for them, and re-layouts, per_device(): values = jnp.take_along_axis(preactivation, clipped_activation, axis=1)  50.3 us
    slice x1, local copies, waits for them, and re-layouts, per_device(): full_table[layer_idx]  47.4 us
    psum x1, blocking collectives, per_device(): scores = lax.psum(score_terms, 'tok').astype(jnp.bfloat16)  31.5 us
    gather x2, local copies, waits for them, and re-layouts, per_device(): jnp.take(full_table[layer_idx], clamped_there[layer_idx], axis=0)  22.1 us
    squeeze x2, local copies, waits for them, and re-layouts, per_device(): full_table[layer_idx]  12.2 us
    dot_general x2, matrix products, accumulate(): return jnp.dot(segment, weights_now, preferred_element_type=jnp.float32)  11.6 us
  transfers between devices with their start and end apart: 6, of which 3 were waited for; matrix products, arithmetic and copies ran while one was open for 19% of the time, Pallas kernels for 0%

commit v1 on v0

--- a/solution.py
+++ b/solution.py
@@ -17,7 +17,7 @@
     layers = residual.shape[0]
     feat_rows = enc_weight.shape[2]
     width_part = dec_sum.shape[2]
-    whole_rows = lax.psum(partial_rows, ("tok", "feat"))
+    whole_rows = lax.psum(lax.psum(partial_rows, "tok"), "feat")
     directions = (whole_rows * norm_gain[None, :]).astype(jnp.bfloat16)
     direction_slice = lax.dynamic_slice_in_dim(directions, tok_pos * width_part, width_part, 1)
     targets = direction_slice.shape[0]

time: 388 us -> 407 us (1.049)
  waiting for transfers between devices: 164 us -> 185 us
    all_gather x2, waiting for transfers between devices: 0.03 us -> 12.6 us  [per_device(): lax.all_gather(residual[layer_idx], 'feat', axis=1, tiled=True)]
    all_gather x1, waiting for transfers between devices: 0.03 us -> 5.65 us  [per_device(): lax.all_gather(scores, 'feat', axis=1, tiled=True)]
    psum x1 -> x2, waiting for transfers between devices: 149 us -> 151 us  [per_device(): whole_rows = lax.psum(lax.psum(partial_rows, 'tok'), 'feat')]
  transfers between devices with their start and end apart: 6 -> 7, of which waited for: 3 -> 6; matrix products, arithmetic and copies ran while one was open for 19% -> 18% of each run, Pallas kernels for 0% -> 0%
where the time goes in v1:
time: 407 us; the launch traced here: 405 us
  waiting for transfers between devices  185 us (45%)
  local copies, waits for them, and re-layouts  142 us (35%)
  blocking collectives  30.7 us (8%)
  matrix products  18.4 us (5%)
  between operations  13.5 us (3%)
  starting transfers between devices  9.25 us (2%)
  other arithmetic  6.42 us (2%)
    psum x2, waiting for transfers between devices, per_device(): whole_rows = lax.psum(lax.psum(partial_rows, 'tok'), 'feat')  151 us
    gather x10, local copies, waits for them, and re-layouts, per_device(): values = jnp.take_along_axis(preactivation, clipped_activation, axis=1)  50.3 us
    slice x1, local copies, waits for them, and re-layouts, per_device(): full_table[layer_idx]  47.4 us
    psum x1, blocking collectives, per_device(): scores = lax.psum(score_terms, 'tok').astype(jnp.bfloat16)  30.7 us
    gather x2, local copies, waits for them, and re-layouts, per_device(): jnp.take(full_table[layer_idx], clamped_there[layer_idx], axis=0)  22.1 us
    all_gather x2, waiting for transfers between devices, per_device(): lax.all_gather(residual[layer_idx], 'feat', axis=1, tiled=True)  12.6 us
    squeeze x2, local copies, waits for them, and re-layouts, per_device(): full_table[layer_idx]  12.2 us
    dot_general x2, matrix products, accumulate(): return jnp.dot(segment, weights_now, preferred_element_type=jnp.float32)  11.5 us
  transfers between devices with their start and end apart: 7, of which 6 were waited for; matrix products, arithmetic and copies ran while one was open for 18% of the time, Pallas kernels for 0%

profile of v1, /device:TPU:0, one launch (start us, length us, event | category | flops | bytes accessed | tf_op | source)
XLA Modules:
  0.0 405.3 jit_solution(8612751963921239789)
XLA Ops:
  7.3 5.5 %fusion.18 = f32[64,3584]{1,0:T(8,128)} fusion(bf16[1024,3584]{1,0:T(8,128)(2,1)} %param.16, s32[64]{0:T(128)S(1)} %broadcast_subtract_fusion), kind=kOutput, calls=%fused_computation.22 | convolution fusion | flops 469827584 | bytes 8257792 | tf_op jit(solution)/shard_map/dot_general | solution.py:16
  12.9 65.1 %all-reduce.4.cloned.1.call-done = f32[64,3584]{1,0:T(8,128)} async-done(((f32[64,3584]{1,0:T(8,128)}), f32[64,3584]{1,0:T(8,128)}) %all-reduce.4.cloned.1.call-update) | async-done | bytes 917520 | tf_op jit(solution)/shard_map/psum | solution.py:20
  80.2 86.3 %all-reduce.6.cloned.1.call-done = f32[64,3584]{1,0:T(8,128)} async-done(((f32[64,3584]{1,0:T(8,128)}), f32[64,3584]{1,0:T(8,128)}) %all-reduce.6.cloned.1.call-update) | async-done | bytes 917520 | tf_op jit(solution)/shard_map/psum | solution.py:20
  166.5 1.4 convolution_bitcast_fusion
  168.8 30.7 %all-reduce.7 = bf16[2,65536]{1,0:T(2,128)(2,1)} all-reduce(f32[2,65536]{1,0:T(2,128)S(1)} %reshape.38), channel_id=1, replica_groups=mesh['tok'=8,'feat'=16] {'tok'}, use_global_device_ids=true, to_apply=%region_2.4 | all-reduce | flops 131072 | bytes 786432 | tf_op jit(solution)/shard_map/psum | solution.py:28
  200.7 4.1 %all-to-all-start.1 = ((s32[16,1,384]{2,1,0:T(1,128)}), s32[16,1,384]{2,1,0:T(1,128)S(1)}, u32[]{:S(2)}, u32[]{:S(2)}) async-start(s32[16,1,384]{2,1,0:T(1,128)} %reshape.105), calls=%async_computation.1 | async-start | bytes 49152 | tf_op jit(solution)/shard_map/all_to_all | solution.py:56
  205.4 7.1 %all-to-all-done.1 = s32[16,1,384]{2,1,0:T(1,128)S(1)} async-done(((s32[16,1,384]{2,1,0:T(1,128)}), s32[16,1,384]{2,1,0:T(1,128)S(1)}, u32[]{:S(2)}, u32[]{:S(2)}) %all-to-all-start.1) | async-done | bytes 24608 | tf_op jit(solution)/shard_map/all_to_all | solution.py:56
  214.8 5.7 %fusion.13 = f32[256,1024]{1,0:T(8,128)S(1)} fusion(bf16[2,3584,1024]{2,1,0:T(8,128)(2,1)} %param.13, bf16[1,256,3584]{1,2,0:T(8,128)(2,1)} %all-gather.10.cloned.1.call-done, f32[1024]{0:T(1024)S(1)} %bitcast.120), kind=kOutput, calls=%fused_computation.17 | convolution fusion | flops 1879310336 | bytes 10227712 | tf_op jit(solution)/shard_map/dot_general | solution.py:35
  220.5 24.7 %gather_fusion.1 = f32[3072]{0:T(1024)S(1)} fusion(f32[256,1024]{1,0:T(8,128)S(1)} %fusion.13, s32[3072]{0:T(1024)S(1)} %reshape.90), kind=kCustom, calls=%fused_computation.2.clone | custom fusion | bytes 49152 | tf_op jit(solution)/shard_map/jit(take_along_axis)/gather | solution.py:47
  245.5 12.6 %all-gather.8.cloned.1.call-done = bf16[1,256,3584]{1,2,0:T(8,128)(2,1)} async-done(((bf16[1,256,224]{1,2,0:T(8,128)(2,1)}), bf16[1,256,3584]{1,2,0:T(8,128)(2,1)}) %all-gather.8.cloned.1.call-update) | async-done | bytes 1835024 | tf_op jit(solution)/shard_map/all_gather | solution.py:40
  258.0 5.7 %fusion.8 = f32[256,1024]{1,0:T(8,128)S(1)} fusion(bf16[2,3584,1024]{2,1,0:T(8,128)(2,1)} %param.13, bf16[1,256,3584]{1,2,0:T(8,128)(2,1)} %all-gather.8.cloned.1.call-done, f32[1024]{0:T(1024)S(1)} %bitcast.119), kind=kOutput, calls=%fused_computation.16 | convolution fusion | flops 1879310336 | bytes 10227712 | tf_op jit(solution)/shard_map/dot_general | solution.py:35
  263.7 24.7 %gather_fusion = f32[3072]{0:T(1024)S(1)} fusion(f32[256,1024]{1,0:T(8,128)S(1)} %fusion.8, s32[3072]{0:T(1024)S(1)} %reshape.85), kind=kCustom, calls=%fused_computation.clone | custom fusion | bytes 49152 | tf_op jit(solution)/shard_map/jit(take_along_axis)/gather | solution.py:47
  289.9 5.0 %all-to-all-start = ((f32[16,1,384]{2,1,0:T(1,128)}), f32[16,1,384]{2,1,0:T(1,128)S(1)}, u32[]{:S(2)}, u32[]{:S(2)}) async-start(f32[16,1,384]{2,1,0:T(1,128)} %reshape.107), calls=%async_computation | async-start | bytes 49152 | tf_op jit(solution)/shard_map/all_to_all | solution.py:55
  294.9 7.8 %all-to-all-done = f32[16,1,384]{2,1,0:T(1,128)S(1)} async-done(((f32[16,1,384]{2,1,0:T(1,128)}), f32[16,1,384]{2,1,0:T(1,128)S(1)}, u32[]{:S(2)}, u32[]{:S(2)}) %all-to-all-start) | async-done | bytes 24608 | tf_op jit(solution)/shard_map/all_to_all | solution.py:55
  305.3 5.6 %all-gather.6.cloned.1.call-done = bf16[2,1048576]{1,0:T(2,128)(2,1)} async-done(((bf16[2,65536]{1,0:T(2,128)(2,1)}), bf16[2,1048576]{1,0:T(2,128)(2,1)}) %all-gather.6.cloned.1.call-update) | async-done | bytes 4194320 | tf_op jit(solution)/shard_map/all_gather | solution.py:52
  311.0 47.4 %slice_reduce_fusion.1 = (bf16[1048576]{0:T(1024)(128)(2,1)}, bf16[1048576]{0:T(1024)(128)(2,1)}) fusion(bf16[2,1048576]{1,0:T(2,128)(2,1)} %all-gather.6.cloned.1.call-done), kind=kLoop, calls=%fused_computation.11 | loop fusion | bytes 8388608 | tf_op jit(solution)/shard_map/slice | solution.py:61
  358.4 6.1 %squeeze.32 = bf16[16384,64]{1,0:T(8,128)(2,1)} reshape(bf16[1048576]{0:T(1024)(128)(2,1)} %get-tuple-element.8) | data formatting | bytes 4194304 | tf_op jit(solution)/shard_map/squeeze | solution.py:61
  364.5 11.0 %gather_fusion.3 = bf16[3072,64]{1,0:T(8,128)(2,1)S(1)} fusion(bf16[16384,64]{1,0:T(8,128)(2,1)} %squeeze.32, s32[3072]{0:T(1024)S(1)} %broadcast_clamp_fusion), kind=kCustom, calls=%fused_computation.3.clone | custom fusion | bytes 798720 | tf_op jit(solution)/shard_map/jit(_take)/gather | solution.py:61
  375.5 1.1 multiply_convert_fusion
  376.6 1.4 stack_reshape.7
  378.0 6.1 %squeeze.30 = bf16[16384,64]{1,0:T(8,128)(2,1)} reshape(bf16[1048576]{0:T(1024)(128)(2,1)} %get-tuple-element.6) | data formatting | bytes 4194304 | tf_op jit(solution)/shard_map/squeeze | solution.py:61
  384.0 11.0 %gather_fusion.2 = bf16[3072,64]{1,0:T(8,128)(2,1)S(1)} fusion(bf16[16384,64]{1,0:T(8,128)(2,1)} %squeeze.30, s32[3072]{0:T(1024)S(1)} %broadcast_clamp_fusion.1), kind=kCustom, calls=%fused_computation.1.clone | custom fusion | bytes 798720 | tf_op jit(solution)/shard_map/jit(_take)/gather | solution.py:61
  395.1 1.1 multiply_convert_fusion.1
  396.8 1.9 pad_maximum_fusion
  (64 shorter events, 12.7 us)
Async XLA Ops:
  6.5 160.0 %copy-start = (bf16[2,1024,448]{1,2,0:T(8,128)(2,1)S(1)}, bf16[2,1024,448]{1,2,0:T(8,128)(2,1)}, u32[]{:S(2)}) copy-start(bf16[2,1024,448]{1,2,0:T(8,128)(2,1)} %param.15) | copy-start | bytes 5505028
  6.5 71.5 %all-reduce.4.cloned.1.call-start = ((), (), s32[]{:S(2)}) async-start(), calls=%async_computation.2 | async-start | bytes 1835008 | tf_op jit(solution)/shard_map/psum | solution.py:20
  7.3 70.8 %copy-start.1 = (bf16[2,256,224]{1,2,0:T(8,128)(2,1)S(1)}, bf16[2,256,224]{1,2,0:T(8,128)(2,1)}, u32[]{:S(2)}) copy-start(bf16[2,256,224]{1,2,0:T(8,128)(2,1)} %param.12) | copy-start | bytes 688132
  12.9 153.7 %all-reduce.6.cloned.1.call-start = ((), (), s32[]{:S(2)}) async-start(), calls=%async_computation.3 | async-start | bytes 1835008 | tf_op jit(solution)/shard_map/psum | solution.py:20
  78.0 136.7 %all-gather.10.cloned.1.call-start = ((), (), s32[]{:S(2)}) async-start(), calls=%async_computation.6 | async-start | bytes 1949696 | tf_op jit(solution)/shard_map/all_gather | solution.py:40
  78.8 179.2 %all-gather.8.cloned.1.call-start = ((), (), s32[]{:S(2)}) async-start(), calls=%async_computation.5 | async-start | bytes 1949696 | tf_op jit(solution)/shard_map/all_gather | solution.py:40
  79.4 231.6 %all-gather.6.cloned.1.call-start = ((), (), s32[]{:S(2)}) async-start(), calls=%async_computation.4 | async-start | bytes 4456448 | tf_op jit(solution)/shard_map/all_gather | solution.py:52
  167.9 31.6 %copy-start.2 = (s32[2,256,12]{1,0,2:T(2,128)S(1)}, s32[2,256,12]{1,0,2:T(2,128)}, u32[]{:S(2)}) copy-start(s32[2,256,12]{1,0,2:T(2,128)} %param.19) | copy-start | bytes 73732
  167.9 37.0 %copy-start.3 = (f32[2,1024]{1,0:T(2,128)S(1)}, f32[2,1024]{1,0:T(2,128)}, u32[]{:S(2)}) copy-start(f32[2,1024]{1,0:T(2,128)} %param.14) | copy-start | bytes 24580
  200.7 11.8 %all-to-all-start.1 = ((s32[16,1,384]{2,1,0:T(1,128)}), s32[16,1,384]{2,1,0:T(1,128)S(1)}, u32[]{:S(2)}, u32[]{:S(2)}) async-start(s32[16,1,384]{2,1,0:T(1,128)} %reshape.105), calls=%async_computation.1 | async-start | bytes 49152 | tf_op jit(solution)/shard_map/all_to_all | solution.py:56
  289.9 12.8 %all-to-all-start = ((f32[16,1,384]{2,1,0:T(1,128)}), f32[16,1,384]{2,1,0:T(1,128)S(1)}, u32[]{:S(2)}, u32[]{:S(2)}) async-start(f32[16,1,384]{2,1,0:T(1,128)} %reshape.107), calls=%async_computation | async-start | bytes 49152 | tf_op jit(solution)/shard_map/all_to_all | solution.py:55
Sparse Core Ops, SparseCore 0:
  13.0 64.9 all-reduce.3
  81.3 85.1 all-reduce.5
  168.7 43.4 all-gather.9
  214.3 43.6 all-gather.7
  260.0 50.9 all-gather.5
